TPU v7x, 32 devices: a whole 2x2x4 slice. The times are simulated.
32 devices in a mesh: str: 8 (over z, x), fac: 4 (over y, core).
Axes of the slice: x: 2, y: 2, z: 4, core: 2. Of those that a mesh axis runs over, the one named last changes fastest.
Arguments:
- amplitudes: bfloat16 [2, 4096, 4096], P(None, 'str'), may hold values from -6 to 6
- beta_index: int32 [2, 32, 12], replicated, may hold values from 0 to 31, all different within a row; in each aligned block of 32 rows (0 to 31, 32 to 63, ..., all dimensions but the last counted through in order) at most 24 rows name the same one
- beta_tile: int32 [2, 12], replicated, may hold values from 0 to 15
- beta_flip: int32 [2, 4096], replicated, may hold values 0 or 1
- alpha_index: int32 [2, 32, 12], replicated, may hold values from 0 to 31, all different within a row; in each aligned block of 32 rows (0 to 31, 32 to 63, ..., all dimensions but the last counted through in order) at most 24 rows name the same one
- alpha_tile: int32 [2, 12], replicated, may hold values from 0 to 15
- alpha_flip: int32 [2, 4096], replicated, may hold values 0 or 1
- beta_tiles: bfloat16 [16, 128, 128], replicated, may hold values from -0.15625 to 0.15625
- alpha_tiles: bfloat16 [16, 128, 128], replicated, may hold values from -0.109375 to 0.109375
Outputs:
- sigma: float32 [2, 4096, 4096], P(None, 'fac', 'str')
Inputs may be any that keep to these rules, and one draw needn't show every extreme that they name: `beta_index`: each block row of one factor's beta operator names 12 different block columns; within one factor's operator no block column is named by more than 24 block rows, and in some factor one column is named by exactly 24. `alpha_index`: each block row of one factor's alpha operator names 12 different block columns; within one factor's operator no block column is named by more than 24 block rows, and in some factor one column is named by exactly 24.
All inputs are finite; a program needn't handle non-finite values.
Results may differ from a plain program's by a relative error of at most 0.012.
Values may be sent and summed in bfloat16 or wider, within the bound.
A program may use at most 128 MiB of HBM per device.

v0:
```python
import jax
import jax.numpy as jnp
from jax import lax
from jax.sharding import PartitionSpec as P


def apply_beta(amplitudes, block_ids, tile_ids, flips, tile_table):
    part_count, height, column_count = amplitudes.shape
    tile_size = tile_table.shape[1]
    block_count = column_count // tile_size
    signs = (1 - 2 * flips).astype(jnp.bfloat16)
    signed = amplitudes * signs[None, None, :]
    blocks = signed.reshape(part_count, height, block_count, tile_size)
    weights = tile_table[tile_ids]
    group_size = block_count // 4
    pieces = []
    for group_id in range(4):
        lower = group_id * group_size
        chosen = block_ids[lower : lower + group_size]
        gathered = blocks[:, :, chosen]
        pieces.append(
            jnp.einsum(
                "pajkc,krc->pajr", gathered, weights, preferred_element_type=jnp.float32
            ).astype(jnp.bfloat16)
        )
    return jnp.concatenate(pieces, axis=2).reshape(part_count, height, column_count)


def apply_alpha(half, block_ids, tile_ids, flips, tile_table):
    part_count, total, column_count = half.shape
    tile_size = tile_table.shape[1]
    block_count = total // tile_size
    signs = (1 - 2 * flips).astype(jnp.bfloat16)
    signed = half * signs[None, :, None]
    blocks = signed.reshape(part_count, block_count, tile_size, column_count)
    weights = tile_table[tile_ids]
    group_size = block_count // 4
    pieces = []
    for group_id in range(4):
        lower = group_id * group_size
        chosen = block_ids[lower : lower + group_size]
        gathered = blocks[:, chosen]
        pieces.append(
            jnp.einsum(
                "pjkcn,krc->pjrn", gathered, weights, preferred_element_type=jnp.float32
            ).astype(jnp.bfloat16)
        )
    return jnp.concatenate(pieces, axis=1).reshape(part_count, total, column_count)


def local(
    amplitudes,
    beta_index,
    beta_tile,
    beta_flip,
    alpha_index,
    alpha_tile,
    alpha_flip,
    beta_tiles,
    alpha_tiles,
):
    position = lax.axis_index("fac")
    factor = position // 2
    part = position % 2
    own_part = lax.dynamic_index_in_dim(amplitudes, part, 0, keepdims=True)
    beta_ids = lax.dynamic_index_in_dim(beta_index, factor, 0, keepdims=False)
    beta_kinds = lax.dynamic_index_in_dim(beta_tile, factor, 0, keepdims=False)
    beta_signs = lax.dynamic_index_in_dim(beta_flip, factor, 0, keepdims=False)
    half = apply_beta(own_part, beta_ids, beta_kinds, beta_signs, beta_tiles)
    alpha_ids = lax.dynamic_index_in_dim(alpha_index, factor, 0, keepdims=False)
    alpha_kinds = lax.dynamic_index_in_dim(alpha_tile, factor, 0, keepdims=False)
    alpha_signs = lax.dynamic_index_in_dim(alpha_flip, factor, 0, keepdims=False)
    mixed = apply_alpha(
        lax.all_to_all(half, "str", split_axis=2, concat_axis=1, tiled=True),
        alpha_ids,
        alpha_kinds,
        alpha_signs,
        alpha_tiles,
    )
    mixed = lax.optimization_barrier(mixed)
    selector = (jnp.arange(2) == part)[:, None, None]
    padded = jnp.where(selector, mixed.astype(jnp.float32), 0.0)
    return lax.psum_scatter(
        padded.astype(jnp.bfloat16), "fac", scatter_dimension=1, tiled=True
    ).astype(jnp.float32)


def solution(mesh):
    return jax.shard_map(
        local,
        mesh=mesh,
        in_specs=(P(None, "str", None), P(), P(), P(), P(), P(), P(), P(), P()),
        out_specs=P(None, "fac", "str"),
        check_vma=False,
    )
```

profile of v0, /device:TPU:0, one launch (start us, length us, event | category | flops | bytes accessed | tf_op | source)
XLA Modules:
  0.0 445.0 jit_solution(6631989853623679221)
XLA Ops:
  6.5 4.8 %constant_dynamic-slice_fusion.9 = bf16[1,512,4096]{2,1,0:T(8,128)(2,1)} fusion(bf16[2,512,4096]{2,1,0:T(8,128)(2,1)} %param.9, s32[]{:T(128)S(6)} %select_n.134), kind=kLoop, calls=%fused_computation.69 | loop fusion | bytes 8388612 | tf_op jit(solution)/shard_map/jit(dynamic_index_in_dim)/dynamic_slice | solution.py:65
  11.3 6.5 %copy.44 = bf16[1,512,4096]{1,2,0:T(8,128)(2,1)} copy(bf16[1,512,4096]{2,1,0:T(8,128)(2,1)} %constant_dynamic-slice_fusion.9) | data formatting | bytes 8388608
  17.9 4.0 broadcast_multiply_fusion
  21.9 6.4 %copy.28 = bf16[512,32,128]{2,0,1:T(8,128)(2,1)} copy(bf16[512,32,128]{0,2,1:T(8,128)(2,1)} %bitcast.181) | data formatting | bytes 8388608 | tf_op jit(solution)/shard_map/reshape | solution.py:13
  28.8 9.0 %gather_fusion.1 = bf16[96,512,128]{2,1,0:T(8,128)(2,1)} fusion(bf16[512,32,128]{2,0,1:T(8,128)(2,1)} %copy.28, s32[1024]{0:T(1024)S(1)} %pad_clamp_fusion.8), kind=kCustom, calls=%fused_computation.1 | custom fusion | bytes 25166208 | tf_op jit(solution)/shard_map/gather | solution.py:20
  37.8 9.0 %gather_fusion.3 = bf16[96,512,128]{2,1,0:T(8,128)(2,1)} fusion(bf16[512,32,128]{2,0,1:T(8,128)(2,1)} %copy.28, s32[1024]{0:T(1024)S(1)} %pad_clamp_fusion.6), kind=kCustom, calls=%fused_computation.3 | custom fusion | bytes 25166208 | tf_op jit(solution)/shard_map/gather | solution.py:20
  47.5 8.9 %fusion = bf16[1,512,8,128]{1,3,2,0:T(8,128)(2,1)S(1)} fusion(bf16[512,8,12,128]{3,0,2,1:T(8,128)(2,1)} %bitcast.174, bf16[12,128,128]{2,1,0:T(8,128)(2,1)S(1)} %gather_fusion.2), kind=kOutput, calls=%fused_computation.24 | convolution fusion | flops 1611137024 | bytes 14024704 | tf_op jit(solution)/shard_map/pajkc,krc->pajr/dot_general | solution.py:22
  56.3 4.2 fusion.1
  60.8 9.0 %gather_fusion.4 = bf16[96,512,128]{2,1,0:T(8,128)(2,1)} fusion(bf16[512,32,128]{2,0,1:T(8,128)(2,1)} %copy.28, s32[1024]{0:T(1024)S(1)} %pad_clamp_fusion.5), kind=kCustom, calls=%fused_computation.4 | custom fusion | bytes 25166208 | tf_op jit(solution)/shard_map/gather | solution.py:20
  69.8 9.7 %fusion.2 = bf16[1,512,8,128]{1,3,2,0:T(8,128)(2,1)} fusion(bf16[512,8,12,128]{3,0,2,1:T(8,128)(2,1)} %bitcast.177, bf16[12,128,128]{2,1,0:T(8,128)(2,1)S(1)} %gather_fusion.2), kind=kOutput, calls=%fused_computation.26 | convolution fusion | flops 1611137024 | bytes 14024704 | tf_op jit(solution)/shard_map/pajkc,krc->pajr/dot_general | solution.py:22
  79.6 9.0 %gather_fusion.5 = bf16[96,512,128]{2,1,0:T(8,128)(2,1)} fusion(bf16[512,32,128]{2,0,1:T(8,128)(2,1)} %copy.28, s32[1024]{0:T(1024)S(1)} %pad_clamp_fusion.4), kind=kCustom, calls=%fused_computation.5 | custom fusion | bytes 25166208 | tf_op jit(solution)/shard_map/gather | solution.py:20
  88.6 8.8 %fusion.3 = bf16[1,512,8,128]{1,3,2,0:T(8,128)(2,1)S(1)} fusion(bf16[512,8,12,128]{3,0,2,1:T(8,128)(2,1)} %bitcast.176, bf16[12,128,128]{2,1,0:T(8,128)(2,1)S(1)} %gather_fusion.2), kind=kOutput, calls=%fused_computation.27 | convolution fusion | flops 1611137024 | bytes 14024704 | tf_op jit(solution)/shard_map/pajkc,krc->pajr/dot_general | solution.py:22
  98.0 36.5 %copy.56 = bf16[1,512,4096]{1,0,2:T(2,128)(2,1)} copy(bf16[1,512,4096]{1,2,0:T(8,128)(2,1)S(1)} %bitcast.178) | data formatting | bytes 8388608 | tf_op jit(solution)/shard_map/reshape | solution.py:26
  135.0 28.5 %reduce.4 = bf16[4096,512]{1,0:T(8,128)(2,1)} reduce(bf16[4096,1,512]{2,1,0:T(2,128)(2,1)} %bitcast.172, bf16[]{:T(256)} %broadcast.272), dimensions={1}, to_apply=%bitcast.167.reduce_sub_computation | reduce | bytes 8388610
  163.5 7.9 %reshape.535 = bf16[8,2,131072]{2,1,0:T(2,128)(2,1)} reshape(bf16[4096,512]{1,0:T(8,128)(2,1)} %reduce.4) | data formatting | bytes 8388608
  171.4 7.3 %all-to-all-start = ((bf16[8,2,131072]{2,1,0:T(2,128)(2,1)}), bf16[8,2,131072]{2,1,0:T(2,128)(2,1)}, u32[]{:S(2)}, u32[]{:S(2)}) async-start(bf16[8,2,131072]{2,1,0:T(2,128)(2,1)} %reshape.535), calls=%async_computation | async-start | bytes 8388608 | tf_op jit(solution)/shard_map/all_to_all | solution.py:74
  180.3 91.7 %all-to-all-done = bf16[8,2,131072]{2,1,0:T(2,128)(2,1)} async-done(((bf16[8,2,131072]{2,1,0:T(2,128)(2,1)}), bf16[8,2,131072]{2,1,0:T(2,128)(2,1)}, u32[]{:S(2)}, u32[]{:S(2)}) %all-to-all-start) | async-done | bytes 4194336 | tf_op jit(solution)/shard_map/all_to_all | solution.py:74
  272.0 8.8 %reshape.536 = bf16[4096,1,512]{2,1,0:T(2,128)(2,1)} reshape(bf16[8,2,131072]{2,1,0:T(2,128)(2,1)} %all-to-all-done) | data formatting | bytes 8388608
  280.8 6.6 %copy.43 = bf16[1,512,4096]{1,2,0:T(8,128)(2,1)} copy(bf16[1,512,4096]{1,0,2:T(2,128)(2,1)} %bitcast.173) | data formatting | bytes 8388608
  287.4 6.5 %copy.33 = bf16[1,8,512,512]{3,2,1,0:T(8,128)(2,1)} copy(bf16[1,8,512,512]{2,3,1,0:T(8,128)(2,1)} %bitcast.179) | data formatting | bytes 8388608 | tf_op jit(solution)/shard_map/all_to_all | solution.py:74
  293.9 3.9 multiply_bitcast_fusion
  297.8 9.0 %gather_fusion.6 = bf16[96,128,512]{2,1,0:T(8,128)(2,1)} fusion(bf16[32,128,512]{2,1,0:T(8,128)(2,1)} %multiply_bitcast_fusion, s32[1024]{0:T(1024)S(1)} %pad_clamp_fusion.3), kind=kCustom, calls=%fused_computation.6 | custom fusion | bytes 25166208 | tf_op jit(solution)/shard_map/gather | solution.py:42
  306.8 9.0 %gather_fusion.7 = bf16[96,128,512]{2,1,0:T(8,128)(2,1)} fusion(bf16[32,128,512]{2,1,0:T(8,128)(2,1)} %multiply_bitcast_fusion, s32[1024]{0:T(1024)S(1)} %pad_clamp_fusion.2), kind=kCustom, calls=%fused_computation.7 | custom fusion | bytes 25166208 | tf_op jit(solution)/shard_map/gather | solution.py:42
  315.8 5.9 %fusion.4 = bf16[1,8,128,512]{3,2,1,0:T(8,128)(2,1)S(1)} fusion(bf16[8,12,128,512]{3,2,1,0:T(8,128)(2,1)} %bitcast.168, bf16[12,128,128]{2,1,0:T(8,128)(2,1)S(1)} %gather_fusion), kind=kOutput, calls=%fused_computation.28 | convolution fusion | flops 1611137024 | bytes 14024704 | tf_op jit(solution)/shard_map/pjkcn,krc->pjrn/dot_general | solution.py:44
  324.0 3.0 fusion.5
  327.0 9.0 %gather_fusion.8 = bf16[96,128,512]{2,1,0:T(8,128)(2,1)} fusion(bf16[32,128,512]{2,1,0:T(8,128)(2,1)} %multiply_bitcast_fusion, s32[1024]{0:T(1024)S(1)} %pad_clamp_fusion.1), kind=kCustom, calls=%fused_computation.8 | custom fusion | bytes 25166208 | tf_op jit(solution)/shard_map/gather | solution.py:42
  336.0 6.7 %fusion.6 = bf16[1,8,128,512]{3,2,1,0:T(8,128)(2,1)} fusion(bf16[8,12,128,512]{3,2,1,0:T(8,128)(2,1)} %bitcast.171, bf16[12,128,128]{2,1,0:T(8,128)(2,1)S(1)} %gather_fusion), kind=kOutput, calls=%fused_computation.30 | convolution fusion | flops 1611137024 | bytes 14024704 | tf_op jit(solution)/shard_map/pjkcn,krc->pjrn/dot_general | solution.py:44
  342.6 9.0 %gather_fusion.9 = bf16[96,128,512]{2,1,0:T(8,128)(2,1)} fusion(bf16[32,128,512]{2,1,0:T(8,128)(2,1)} %multiply_bitcast_fusion, s32[1024]{0:T(1024)S(1)} %pad_clamp_fusion), kind=kCustom, calls=%fused_computation.9 | custom fusion | bytes 25166208 | tf_op jit(solution)/shard_map/gather | solution.py:42
  351.7 5.9 %fusion.7 = bf16[1,8,128,512]{3,2,1,0:T(8,128)(2,1)S(1)} fusion(bf16[8,12,128,512]{3,2,1,0:T(8,128)(2,1)} %bitcast.170, bf16[12,128,128]{2,1,0:T(8,128)(2,1)S(1)} %gather_fusion), kind=kOutput, calls=%fused_computation.31 | convolution fusion | flops 1611137024 | bytes 14024704 | tf_op jit(solution)/shard_map/pjkcn,krc->pjrn/dot_general | solution.py:44
  358.2 5.1 %select_convert_fusion = bf16[2,4096,512]{2,1,0:T(8,128)(2,1)} fusion(bf16[4096,512]{1,0:T(8,128)(2,1)S(1)} %bitcast.182, pred[2]{0:T(512)(128)(4,1)S(1)} %iota_compare_fusion), kind=kLoop, calls=%fused_computation.10 | loop fusion | flops 4194304 | bytes 12582914 | tf_op jit(solution)/shard_map/convert_element_type | solution.py:84
  363.3 70.7 %reduce-scatter.2.cloned.1.call-done = bf16[2,1024,512]{2,1,0:T(8,128)(2,1)} async-done(((bf16[2,4096,512]{2,1,0:T(8,128)(2,1)}), bf16[2,1024,512]{2,1,0:T(8,128)(2,1)}) %reduce-scatter.2.cloned.1.call-update) | async-done | bytes 2097168 | tf_op jit(solution)/shard_map/reduce_scatter | solution.py:83
  433.9 4.2 convert_element_type.112
  (70 shorter events, 7.1 us)
Async XLA Ops:
  6.5 40.3 %copy-start = (bf16[16,128,128]{2,1,0:T(8,128)(2,1)S(1)}, bf16[16,128,128]{2,1,0:T(8,128)(2,1)}, u32[]{:S(2)}) copy-start(bf16[16,128,128]{2,1,0:T(8,128)(2,1)} %param.16) | copy-start | bytes 1572868
  6.5 11.2 %copy-start.10 = (s32[2,4096]{1,0:T(2,128)S(1)}, s32[2,4096]{1,0:T(2,128)}, u32[]{:S(2)}) copy-start(s32[2,4096]{1,0:T(2,128)} %param.15) | copy-start | bytes 98308
  6.5 11.2 %copy-start.11 = (s32[2,4096]{1,0:T(2,128)S(1)}, s32[2,4096]{1,0:T(2,128)}, u32[]{:S(2)}) copy-start(s32[2,4096]{1,0:T(2,128)} %param.12) | copy-start | bytes 98308
  17.9 10.4 %copy-start.8 = (s32[2,32,12]{1,0,2:T(2,128)S(1)}, s32[2,32,12]{1,0,2:T(2,128)}, u32[]{:S(2)}) copy-start(s32[2,32,12]{1,0,2:T(2,128)} %param.10) | copy-start | bytes 9220
  17.9 10.8 %copy-start.12 = (s32[2,12]{1,0:T(2,128)S(1)}, s32[2,12]{1,0:T(2,128)}, u32[]{:S(2)}) copy-start(s32[2,12]{1,0:T(2,128)} %param.14) | copy-start | bytes 292
  17.9 10.8 %copy-start.13 = (s32[2,12]{1,0:T(2,128)S(1)}, s32[2,12]{1,0:T(2,128)}, u32[]{:S(2)}) copy-start(s32[2,12]{1,0:T(2,128)} %param.11) | copy-start | bytes 292
  47.4 8.9 %copy-start.3 = (bf16[96,512,128]{2,1,0:T(8,128)(2,1)S(1)}, bf16[96,512,128]{2,1,0:T(8,128)(2,1)}, u32[]{:S(2)}) copy-start(bf16[96,512,128]{2,1,0:T(8,128)(2,1)} %gather_fusion.3) | copy-start | bytes 37748740
  88.6 8.8 %copy-start.6 = (bf16[1,512,8,128]{1,3,2,0:T(8,128)(2,1)S(1)}, bf16[1,512,8,128]{1,3,2,0:T(8,128)(2,1)}, u32[]{:S(2)}) copy-start(bf16[1,512,8,128]{1,3,2,0:T(8,128)(2,1)} %fusion.2) | copy-start | bytes 3145732
  163.5 15.2 %copy-start.9 = (s32[2,32,12]{1,0,2:T(2,128)S(1)}, s32[2,32,12]{1,0,2:T(2,128)}, u32[]{:S(2)}) copy-start(s32[2,32,12]{1,0,2:T(2,128)} %param.13) | copy-start | bytes 9220
  163.5 16.0 %copy-start.7 = (bf16[16,128,128]{2,1,0:T(8,128)(2,1)S(1)}, bf16[16,128,128]{2,1,0:T(8,128)(2,1)}, u32[]{:S(2)}) copy-start(bf16[16,128,128]{2,1,0:T(8,128)(2,1)} %param.17) | copy-start | bytes 1572868
  171.4 100.6 %all-to-all-start = ((bf16[8,2,131072]{2,1,0:T(2,128)(2,1)}), bf16[8,2,131072]{2,1,0:T(2,128)(2,1)}, u32[]{:S(2)}, u32[]{:S(2)}) async-start(bf16[8,2,131072]{2,1,0:T(2,128)(2,1)} %reshape.535), calls=%async_computation | async-start | bytes 8388608 | tf_op jit(solution)/shard_map/all_to_all | solution.py:74
  178.7 255.2 %reduce-scatter.2.cloned.1.call-start = ((), (), s32[]{:S(2)}) async-start(), calls=%async_computation.2 | async-start | bytes 10485760 | tf_op jit(solution)/shard_map/reduce_scatter | solution.py:83
  315.8 8.2 %copy-start.2 = (bf16[96,128,512]{2,1,0:T(8,128)(2,1)S(1)}, bf16[96,128,512]{2,1,0:T(8,128)(2,1)}, u32[]{:S(2)}) copy-start(bf16[96,128,512]{2,1,0:T(8,128)(2,1)} %gather_fusion.7) | copy-start | bytes 37748740
  351.7 5.9 %copy-start.4 = (bf16[1,8,128,512]{3,2,1,0:T(8,128)(2,1)S(1)}, bf16[1,8,128,512]{3,2,1,0:T(8,128)(2,1)}, u32[]{:S(2)}) copy-start(bf16[1,8,128,512]{3,2,1,0:T(8,128)(2,1)} %fusion.5) | copy-start | bytes 3145732
  351.7 5.9 %copy-start.5 = (bf16[1,8,128,512]{3,2,1,0:T(8,128)(2,1)S(1)}, bf16[1,8,128,512]{3,2,1,0:T(8,128)(2,1)}, u32[]{:S(2)}) copy-start(bf16[1,8,128,512]{3,2,1,0:T(8,128)(2,1)} %fusion.6) | copy-start | bytes 3145732
  358.1 80.0 %copy-start.1 = (bf16[16,128,128]{2,1,0:T(8,128)(2,1)S(1)}, bf16[16,128,128]{2,1,0:T(8,128)(2,1)}, u32[]{:S(2)}) copy-start(bf16[16,128,128]{2,1,0:T(8,128)(2,1)} %param.16) | copy-start | bytes 1572868
Sparse Core Ops, SparseCore 0:
  363.4 70.5 reduce-scatter.1
where the time goes:
time: 446 us; the launch traced here: 445 us
  local copies, waits for them, and re-layouts  162 us (36%)
  waiting for transfers between devices  162 us (36%)
  matrix products  52.9 us (12%)
  other arithmetic  47.1 us (11%)
  between operations  13.7 us (3%)
  starting transfers between devices  7.33 us (2%)
    all_to_all x1, waiting for transfers between devices, local(): lax.all_to_all(half, 'str', split_axis=2, concat_axis=1, tiled=True)  91.7 us
    reduce_scatter x1, waiting for transfers between devices, local(): lax.psum_scatter(padded.astype(jnp.bfloat16), 'fac', scatter_dimension=1,...  70.7 us
    reshape x1, local copies, waits for them, and re-layouts, apply_beta(): jnp.concatenate(pieces, axis=2).reshape(part_count, height, column_count)  36.5 us
    gather x4, local copies, waits for them, and re-layouts, apply_beta(): gathered = blocks[:, :, chosen]  36.1 us
    gather x4, local copies, waits for them, and re-layouts, apply_alpha(): gathered = blocks[:, chosen]  36 us
    unnamed x41, local copies, waits for them, and re-layouts  33.3 us
    dot_general x4, matrix products, apply_beta(): jnp.einsum('pajkc,krc->pajr', gathered, weights, preferred_element_type=j...  31.5 us
    unnamed x1, other arithmetic  28.5 us
  transfers between devices with their start and end apart: 2, of which 2 were waited for; matrix products, arithmetic and copies ran while one was open for 0% of the time, Pallas kernels for 0%

commit v1 on v0

--- a/solution.py
+++ b/solution.py
@@ -2,6 +2,29 @@
 import jax.numpy as jnp
 from jax import lax
 from jax.sharding import PartitionSpec as P
+
+
+def cut_along(x, dim, size):
+    before, after = (x.shape[:dim], x.shape[dim + 1 :])
+    return jnp.moveaxis(x.reshape(*before, size, -1, *after), dim, 0)
+
+
+def laid_out(tiles, dim):
+    tiles = jnp.moveaxis(tiles, 0, dim)
+    lengths = tiles.shape
+    return tiles.reshape(*lengths[:dim], lengths[dim] * lengths[dim + 1], *lengths[dim + 2 :])
+
+
+def rotated_exchange(value, axis, split_dim, concat_dim):
+    size, mine = (lax.axis_size(axis), lax.axis_index(axis))
+    parts = cut_along(value, split_dim, size)
+    whole = parts
+    for step in range(1, size):
+        target, source = ((mine + step) % size, (mine - step) % size)
+        sent = lax.dynamic_index_in_dim(parts, target, 0)
+        other = lax.ppermute(sent, axis, [(i, (i + step) % size) for i in range(size)])
+        whole = lax.dynamic_update_slice_in_dim(whole, other, source, axis=0)
+    return laid_out(whole, concat_dim)
 
 
 def apply_beta(amplitudes, block_ids, tile_ids, flips, tile_table):
@@ -71,11 +94,7 @@
     alpha_kinds = lax.dynamic_index_in_dim(alpha_tile, factor, 0, keepdims=False)
     alpha_signs = lax.dynamic_index_in_dim(alpha_flip, factor, 0, keepdims=False)
     mixed = apply_alpha(
-        lax.all_to_all(half, "str", split_axis=2, concat_axis=1, tiled=True),
-        alpha_ids,
-        alpha_kinds,
-        alpha_signs,
-        alpha_tiles,
+        rotated_exchange(half, "str", 2, 1), alpha_ids, alpha_kinds, alpha_signs, alpha_tiles
     )
     mixed = lax.optimization_barrier(mixed)
     selector = (jnp.arange(2) == part)[:, None, None]

time: 446 us -> 361 us (0.81)
  local copies, waits for them, and re-layouts: 162 us -> 121 us
  waiting for transfers between devices: 162 us -> 132 us
  other arithmetic: 47.1 us -> 20.8 us
  starting transfers between devices: 7.33 us -> 18.5 us
    all_to_all x1 -> x0, waiting for transfers between devices: 91.7 us -> none  [local(): lax.all_to_all(half, 'str', split_axis=2, concat_axis=1, tiled=True)]
    reshape x1 -> x0, local copies, waits for them, and re-layouts: 36.5 us -> none  [apply_beta(): jnp.concatenate(pieces, axis=2).reshape(part_count, height, column_count)]
    ppermute x0 -> x7, waiting for transfers between devices: none -> 33 us  [rotated_exchange(): lax.ppermute(sent, axis, [(i, (i + step) % size) for i in range(size)])]
    unnamed x1 -> x0, other arithmetic: 28.5 us -> none
    reduce_scatter x1, waiting for transfers between devices: 70.7 us -> 98.9 us  [local(): lax.psum_scatter(padded.astype(jnp.bfloat16), 'fac', scatter_dimension=1,...]
    unnamed x41 -> x35, local copies, waits for them, and re-layouts: 33.3 us -> 11.5 us
    ppermute x0 -> x7, starting transfers between devices: none -> 18.5 us  [rotated_exchange(): lax.ppermute(sent, axis, [(i, (i + step) % size) for i in range(size)])]
    another operation x0 -> x9, local copies, waits for them, and re-layouts: none -> 11.8 us  [the longest x1 6.47 us: cut_along(): return jnp.moveaxis(x.reshape(*before, size, -1, *after), dim, 0)]
  transfers between devices with their start and end apart: 2 -> 8, of which waited for: 2 -> 3; matrix products, arithmetic and copies ran while one was open for 0% -> 6% of each run, Pallas kernels for 0% -> 0%
where the time goes in v1:
time: 361 us; the launch traced here: 360 us
  waiting for transfers between devices  132 us (37%)
  local copies, waits for them, and re-layouts  121 us (34%)
  matrix products  53.9 us (15%)
  other arithmetic  20.8 us (6%)
  starting transfers between devices  18.5 us (5%)
  between operations  13.7 us (4%)
    reduce_scatter x1, waiting for transfers between devices, local(): lax.psum_scatter(padded.astype(jnp.bfloat16), 'fac', scatter_dimension=1,...  98.9 us
    gather x4, local copies, waits for them, and re-layouts, apply_beta(): gathered = blocks[:, :, chosen]  36.1 us
    gather x4, local copies, waits for them, and re-layouts, apply_alpha(): gathered = blocks[:, chosen]  36.1 us
    ppermute x7, waiting for transfers between devices, rotated_exchange(): lax.ppermute(sent, axis, [(i, (i + step) % size) for i in range(size)])  33 us
    dot_general x4, matrix products, apply_beta(): jnp.einsum('pajkc,krc->pajr', gathered, weights, preferred_element_type=j...  32.5 us
    dot_general x4, matrix products, apply_alpha(): jnp.einsum('pjkcn,krc->pjrn', gathered, weights, preferred_element_type=j...  21.4 us
    ppermute x7, starting transfers between devices, rotated_exchange(): lax.ppermute(sent, axis, [(i, (i + step) % size) for i in range(size)])  18.5 us
    unnamed x35, local copies, waits for them, and re-layouts  11.5 us
  transfers between devices with their start and end apart: 8, of which 3 were waited for; matrix products, arithmetic and copies ran while one was open for 6% of the time, Pallas kernels for 0%

profile of v1, /device:TPU:0, one launch (start us, length us, event | category | flops | bytes accessed | tf_op | source)
XLA Modules:
  0.0 359.6 jit_solution(7498206489567525504)
XLA Ops:
  6.5 4.8 %constant_dynamic-slice_fusion.16 = bf16[1,512,4096]{2,1,0:T(8,128)(2,1)} fusion(bf16[2,512,4096]{2,1,0:T(8,128)(2,1)} %param.9, s32[]{:T(128)S(6)} %select_n.233), kind=kLoop, calls=%fused_computation.73 | loop fusion | bytes 8388612 | tf_op jit(solution)/shard_map/jit(dynamic_index_in_dim)/dynamic_slice | solution.py:88
  11.3 6.5 %copy.49 = bf16[1,512,4096]{1,2,0:T(8,128)(2,1)} copy(bf16[1,512,4096]{2,1,0:T(8,128)(2,1)} %constant_dynamic-slice_fusion.16) | data formatting | bytes 8388608
  17.9 3.9 %broadcast_multiply_fusion = bf16[1,512,4096]{1,2,0:T(8,128)(2,1)} fusion(bf16[1,512,4096]{1,2,0:T(8,128)(2,1)} %copy.49, bf16[4096]{0:T(1024)(128)(2,1)S(1)} %convert_reduce_fusion.1), kind=kLoop, calls=%fused_computation.23 | loop fusion | flops 2097152 | bytes 8396800 | tf_op jit(solution)/shard_map/mul | solution.py:35
  21.8 6.5 %copy.28 = bf16[512,32,128]{2,0,1:T(8,128)(2,1)} copy(bf16[512,32,128]{0,2,1:T(8,128)(2,1)} %bitcast.181) | data formatting | bytes 8388608 | tf_op jit(solution)/shard_map/reshape | solution.py:36
  28.8 9.0 %gather_fusion.1 = bf16[96,512,128]{2,1,0:T(8,128)(2,1)} fusion(bf16[512,32,128]{2,0,1:T(8,128)(2,1)} %copy.28, s32[1024]{0:T(1024)S(1)} %pad_clamp_fusion.8), kind=kCustom, calls=%fused_computation.1 | custom fusion | bytes 25166208 | tf_op jit(solution)/shard_map/gather | solution.py:43
  37.8 9.0 %gather_fusion.3 = bf16[96,512,128]{2,1,0:T(8,128)(2,1)} fusion(bf16[512,32,128]{2,0,1:T(8,128)(2,1)} %copy.28, s32[1024]{0:T(1024)S(1)} %pad_clamp_fusion.6), kind=kCustom, calls=%fused_computation.3 | custom fusion | bytes 25166208 | tf_op jit(solution)/shard_map/gather | solution.py:43
  47.5 8.9 %fusion = bf16[1,512,8,128]{1,3,2,0:T(8,128)(2,1)S(1)} fusion(bf16[512,8,12,128]{3,0,2,1:T(8,128)(2,1)} %bitcast.175, bf16[12,128,128]{2,1,0:T(8,128)(2,1)S(1)} %gather_fusion.2), kind=kOutput, calls=%fused_computation.24 | convolution fusion | flops 1611137024 | bytes 14024704 | tf_op jit(solution)/shard_map/pajkc,krc->pajr/dot_general | solution.py:45
  56.4 4.2 %fusion.1 = bf16[1,512,8,128]{1,3,2,0:T(8,128)(2,1)S(1)} fusion(bf16[512,8,12,128]{3,0,2,1:T(8,128)(2,1)S(1)} %bitcast.176, bf16[12,128,128]{2,1,0:T(8,128)(2,1)S(1)} %gather_fusion.2), kind=kOutput, calls=%fused_computation.25 | convolution fusion | flops 1611137024 | bytes 14024704 | tf_op jit(solution)/shard_map/pajkc,krc->pajr/dot_general | solution.py:45
  60.8 9.0 %gather_fusion.4 = bf16[96,512,128]{2,1,0:T(8,128)(2,1)} fusion(bf16[512,32,128]{2,0,1:T(8,128)(2,1)} %copy.28, s32[1024]{0:T(1024)S(1)} %pad_clamp_fusion.5), kind=kCustom, calls=%fused_computation.4 | custom fusion | bytes 25166208 | tf_op jit(solution)/shard_map/gather | solution.py:43
  69.8 9.8 %fusion.2 = bf16[1,512,8,128]{1,3,2,0:T(8,128)(2,1)} fusion(bf16[512,8,12,128]{3,0,2,1:T(8,128)(2,1)} %bitcast.178, bf16[12,128,128]{2,1,0:T(8,128)(2,1)S(1)} %gather_fusion.2), kind=kOutput, calls=%fused_computation.26 | convolution fusion | flops 1611137024 | bytes 14024704 | tf_op jit(solution)/shard_map/pajkc,krc->pajr/dot_general | solution.py:45
  79.7 9.0 %gather_fusion.5 = bf16[96,512,128]{2,1,0:T(8,128)(2,1)} fusion(bf16[512,32,128]{2,0,1:T(8,128)(2,1)} %copy.28, s32[1024]{0:T(1024)S(1)} %pad_clamp_fusion.4), kind=kCustom, calls=%fused_computation.5 | custom fusion | bytes 25166208 | tf_op jit(solution)/shard_map/gather | solution.py:43
  88.7 9.7 %fusion.3 = bf16[1,512,8,128]{1,3,2,0:T(8,128)(2,1)} fusion(bf16[512,8,12,128]{3,0,2,1:T(8,128)(2,1)} %bitcast.177, bf16[12,128,128]{2,1,0:T(8,128)(2,1)S(1)} %gather_fusion.2), kind=kOutput, calls=%fused_computation.27 | convolution fusion | flops 1611137024 | bytes 14024704 | tf_op jit(solution)/shard_map/pajkc,krc->pajr/dot_general | solution.py:45
  98.4 2.8 pad_maximum_fusion
  106.5 3.0 collective-permute-start
  112.2 2.6 collective-permute-start.2
  116.6 2.7 collective-permute-start.4
  120.1 6.5 %copy.32 = bf16[1,512,8,512]{3,1,2,0:T(8,128)(2,1)} copy(bf16[1,512,8,512]{1,3,2,0:T(8,128)(2,1)} %bitcast.174) | data formatting | bytes 8388608 | tf_op jit(solution)/shard_map/reshape;reshape | solution.py:9
  132.1 5.9 %collective-permute-start.6 = (bf16[1,1,512,512]{3,2,0,1:T(8,128)(2,1)S(1)}, bf16[1,1,512,512]{3,2,0,1:T(8,128)(2,1)S(1)}, u32[]{:S(2)}, u32[]{:S(2)}) collective-permute-start(bf16[1,1,512,512]{3,2,0,1:T(8,128)(2,1)S(1)} %bitcast.188), channel_id=1, source_target_pairs={{0,28},{4,0},{8,4},{12,8},{16,12},{20,16},{24,20},{28,24},{1,29},{... | collective-permute-start | bytes 1572872 | tf_op jit(solution)/shard_map/ppermute | solution.py:25
  139.9 29.9 %collective-permute-done.2 = bf16[1,1,512,512]{3,2,0,1:T(8,128)(2,1)} collective-permute-done((bf16[1,1,512,512]{3,2,0,1:T(8,128)(2,1)S(1)}, bf16[1,1,512,512]{3,2,0,1:T(8,128)(2,1)}, u32[]{:S(2)}, u32[]{:S(2)}) %collective-permute-start.2) | collective-permute-done | bytes 524320 | tf_op jit(solution)/shard_map/ppermute | solution.py:25
  176.2 3.1 collective-permute-done.6
  180.2 3.9 %multiply_bitcast_fusion = bf16[32,128,512]{2,1,0:T(8,128)(2,1)} fusion(bf16[1,32,128,512]{3,2,1,0:T(8,128)(2,1)} %bitcast.180, bf16[32,128]{1,0:T(8,128)(2,1)S(1)} %bitcast.190), kind=kLoop, calls=%fused_computation.14 | loop fusion | flops 2097152 | bytes 8396800 | tf_op jit(solution)/shard_map/mul | solution.py:57
  184.1 9.0 %gather_fusion.6 = bf16[96,128,512]{2,1,0:T(8,128)(2,1)} fusion(bf16[32,128,512]{2,1,0:T(8,128)(2,1)} %multiply_bitcast_fusion, s32[1024]{0:T(1024)S(1)} %pad_clamp_fusion.3), kind=kCustom, calls=%fused_computation.6 | custom fusion | bytes 25166208 | tf_op jit(solution)/shard_map/gather | solution.py:65
  193.1 9.0 %gather_fusion.7 = bf16[96,128,512]{2,1,0:T(8,128)(2,1)} fusion(bf16[32,128,512]{2,1,0:T(8,128)(2,1)} %multiply_bitcast_fusion, s32[1024]{0:T(1024)S(1)} %pad_clamp_fusion.2), kind=kCustom, calls=%fused_computation.7 | custom fusion | bytes 25166208 | tf_op jit(solution)/shard_map/gather | solution.py:65
  202.1 5.9 %fusion.4 = bf16[1,8,128,512]{3,2,1,0:T(8,128)(2,1)S(1)} fusion(bf16[8,12,128,512]{3,2,1,0:T(8,128)(2,1)} %bitcast.169, bf16[12,128,128]{2,1,0:T(8,128)(2,1)S(1)} %gather_fusion), kind=kOutput, calls=%fused_computation.28 | convolution fusion | flops 1611137024 | bytes 14024704 | tf_op jit(solution)/shard_map/pjkcn,krc->pjrn/dot_general | solution.py:67
  210.3 3.0 fusion.5
  213.3 9.0 %gather_fusion.8 = bf16[96,128,512]{2,1,0:T(8,128)(2,1)} fusion(bf16[32,128,512]{2,1,0:T(8,128)(2,1)} %multiply_bitcast_fusion, s32[1024]{0:T(1024)S(1)} %pad_clamp_fusion.1), kind=kCustom, calls=%fused_computation.8 | custom fusion | bytes 25166208 | tf_op jit(solution)/shard_map/gather | solution.py:65
  222.3 6.7 %fusion.6 = bf16[1,8,128,512]{3,2,1,0:T(8,128)(2,1)} fusion(bf16[8,12,128,512]{3,2,1,0:T(8,128)(2,1)} %bitcast.172, bf16[12,128,128]{2,1,0:T(8,128)(2,1)S(1)} %gather_fusion), kind=kOutput, calls=%fused_computation.30 | convolution fusion | flops 1611137024 | bytes 14024704 | tf_op jit(solution)/shard_map/pjkcn,krc->pjrn/dot_general | solution.py:67
  229.0 9.0 %gather_fusion.9 = bf16[96,128,512]{2,1,0:T(8,128)(2,1)} fusion(bf16[32,128,512]{2,1,0:T(8,128)(2,1)} %multiply_bitcast_fusion, s32[1024]{0:T(1024)S(1)} %pad_clamp_fusion), kind=kCustom, calls=%fused_computation.9 | custom fusion | bytes 25166208 | tf_op jit(solution)/shard_map/gather | solution.py:65
  238.0 5.9 %fusion.7 = bf16[1,8,128,512]{3,2,1,0:T(8,128)(2,1)S(1)} fusion(bf16[8,12,128,512]{3,2,1,0:T(8,128)(2,1)} %bitcast.171, bf16[12,128,128]{2,1,0:T(8,128)(2,1)S(1)} %gather_fusion), kind=kOutput, calls=%fused_computation.31 | convolution fusion | flops 1611137024 | bytes 14024704 | tf_op jit(solution)/shard_map/pjkcn,krc->pjrn/dot_general | solution.py:67
  244.5 5.1 %select_convert_fusion = bf16[2,4096,512]{2,1,0:T(8,128)(2,1)} fusion(bf16[4096,512]{1,0:T(8,128)(2,1)S(1)} %bitcast.182, pred[2]{0:T(512)(128)(4,1)S(1)} %iota_compare_fusion), kind=kLoop, calls=%fused_computation.10 | loop fusion | flops 4194304 | bytes 12582914 | tf_op jit(solution)/shard_map/convert_element_type | solution.py:103
  249.7 98.9 %reduce-scatter.2.cloned.1.call-done = bf16[2,1024,512]{2,1,0:T(8,128)(2,1)} async-done(((bf16[2,4096,512]{2,1,0:T(8,128)(2,1)}), bf16[2,1024,512]{2,1,0:T(8,128)(2,1)}) %reduce-scatter.2.cloned.1.call-update) | async-done | bytes 2097168 | tf_op jit(solution)/shard_map/reduce_scatter | solution.py:102
  348.5 4.2 %convert_element_type.112 = f32[2,1024,512]{2,1,0:T(8,128)} convert(bf16[2,1024,512]{2,1,0:T(8,128)(2,1)} %reduce-scatter.2.cloned.1.call-done) | non-fusion elementwise | flops 1048576 | bytes 6291456 | tf_op jit(solution)/shard_map/convert_element_type | solution.py:104
  (90 shorter events, 29.6 us)
Async XLA Ops:
  6.5 40.3 %copy-start = (bf16[16,128,128]{2,1,0:T(8,128)(2,1)S(1)}, bf16[16,128,128]{2,1,0:T(8,128)(2,1)}, u32[]{:S(2)}) copy-start(bf16[16,128,128]{2,1,0:T(8,128)(2,1)} %param.16) | copy-start | bytes 1572868
  6.5 342.0 %reduce-scatter.2.cloned.1.call-start = ((), (), s32[]{:S(2)}) async-start(), calls=%async_computation.1 | async-start | bytes 10485760 | tf_op jit(solution)/shard_map/reduce_scatter | solution.py:102
  11.3 6.5 %copy-start.9 = (s32[2,4096]{1,0:T(2,128)S(1)}, s32[2,4096]{1,0:T(2,128)}, u32[]{:S(2)}) copy-start(s32[2,4096]{1,0:T(2,128)} %param.12) | copy-start | bytes 98308
  21.8 6.5 %copy-start.7 = (s32[2,32,12]{1,0,2:T(2,128)S(1)}, s32[2,32,12]{1,0,2:T(2,128)}, u32[]{:S(2)}) copy-start(s32[2,32,12]{1,0,2:T(2,128)} %param.10) | copy-start | bytes 9220
  21.8 6.8 %copy-start.11 = (s32[2,12]{1,0:T(2,128)S(1)}, s32[2,12]{1,0:T(2,128)}, u32[]{:S(2)}) copy-start(s32[2,12]{1,0:T(2,128)} %param.14) | copy-start | bytes 292
  21.8 6.9 %copy-start.12 = (s32[2,12]{1,0:T(2,128)S(1)}, s32[2,12]{1,0:T(2,128)}, u32[]{:S(2)}) copy-start(s32[2,12]{1,0:T(2,128)} %param.11) | copy-start | bytes 292
  47.5 8.9 %copy-start.4 = (bf16[96,512,128]{2,1,0:T(8,128)(2,1)S(1)}, bf16[96,512,128]{2,1,0:T(8,128)(2,1)}, u32[]{:S(2)}) copy-start(bf16[96,512,128]{2,1,0:T(8,128)(2,1)} %gather_fusion.3) | copy-start | bytes 37748740
  101.2 2.0 copy-start.3
  104.4 14.9 %copy-start.8 = (s32[2,32,12]{1,0,2:T(2,128)S(1)}, s32[2,32,12]{1,0,2:T(2,128)}, u32[]{:S(2)}) copy-start(s32[2,32,12]{1,0,2:T(2,128)} %param.13) | copy-start | bytes 9220
  106.5 22.3 %collective-permute-start = (bf16[1,1,512,512]{3,2,0,1:T(8,128)(2,1)}, bf16[1,1,512,512]{3,2,0,1:T(8,128)(2,1)}, u32[]{:S(2)}, u32[]{:S(2)}) collective-permute-start(bf16[1,1,512,512]{3,2,0,1:T(8,128)(2,1)} %bitcast.187), channel_id=1, source_target_pairs={{0,4},{4,8},{8,12},{12,16},{16,20},{20,24},{24,28},{28,0},{1,5},{5... | collective-permute-start | bytes 1572872 | tf_op jit(solution)/shard_map/ppermute | solution.py:25
  110.4 21.7 %collective-permute-start.1 = (bf16[1,1,512,512]{3,2,0,1:T(8,128)(2,1)}, bf16[1,1,512,512]{3,2,0,1:T(8,128)(2,1)}, u32[]{:S(2)}, u32[]{:S(2)}) collective-permute-start(bf16[1,1,512,512]{3,2,0,1:T(8,128)(2,1)} %bitcast.186), channel_id=1, source_target_pairs={{0,8},{4,12},{8,16},{12,20},{16,24},{20,28},{24,0},{28,4},{1,9},{5... | collective-permute-start | bytes 1572872 | tf_op jit(solution)/shard_map/ppermute | solution.py:25
  112.2 57.5 %collective-permute-start.2 = (bf16[1,1,512,512]{3,2,0,1:T(8,128)(2,1)S(1)}, bf16[1,1,512,512]{3,2,0,1:T(8,128)(2,1)}, u32[]{:S(2)}, u32[]{:S(2)}) collective-permute-start(bf16[1,1,512,512]{3,2,0,1:T(8,128)(2,1)S(1)} %bitcast.185), channel_id=1, source_target_pairs={{0,12},{4,16},{8,20},{12,24},{16,28},{20,0},{24,4},{28,8},{1,13},{... | collective-permute-start | bytes 1572872 | tf_op jit(solution)/shard_map/ppermute | solution.py:25
  115.0 56.6 %collective-permute-start.3 = (bf16[1,1,512,512]{3,2,0,1:T(8,128)(2,1)S(1)}, bf16[1,1,512,512]{3,2,0,1:T(8,128)(2,1)}, u32[]{:S(2)}, u32[]{:S(2)}) collective-permute-start(bf16[1,1,512,512]{3,2,0,1:T(8,128)(2,1)S(1)} %bitcast.184), channel_id=1, source_target_pairs={{0,16},{4,20},{8,24},{12,28},{16,0},{20,4},{24,8},{28,12},{1,17},{... | collective-permute-start | bytes 1572872 | tf_op jit(solution)/shard_map/ppermute | solution.py:25
  116.6 56.9 %collective-permute-start.4 = (bf16[1,1,512,512]{3,2,0,1:T(8,128)(2,1)S(1)}, bf16[1,1,512,512]{3,2,0,1:T(8,128)(2,1)}, u32[]{:S(2)}, u32[]{:S(2)}) collective-permute-start(bf16[1,1,512,512]{3,2,0,1:T(8,128)(2,1)S(1)} %bitcast.183), channel_id=1, source_target_pairs={{0,20},{4,24},{8,28},{12,0},{16,4},{20,8},{24,12},{28,16},{1,21},{... | collective-permute-start | bytes 1572872 | tf_op jit(solution)/shard_map/ppermute | solution.py:25
  120.1 8.6 %copy-start.10 = (s32[2,4096]{1,0:T(2,128)S(1)}, s32[2,4096]{1,0:T(2,128)}, u32[]{:S(2)}) copy-start(s32[2,4096]{1,0:T(2,128)} %param.15) | copy-start | bytes 98308
  128.8 46.6 %collective-permute-start.5 = (bf16[1,1,512,512]{3,2,0,1:T(8,128)(2,1)S(1)}, bf16[1,1,512,512]{3,2,0,1:T(8,128)(2,1)S(1)}, u32[]{:S(2)}, u32[]{:S(2)}) collective-permute-start(bf16[1,1,512,512]{3,2,0,1:T(8,128)(2,1)S(1)} %bitcast.189), channel_id=1, source_target_pairs={{0,24},{4,28},{8,0},{12,4},{16,8},{20,12},{24,16},{28,20},{1,25},{... | collective-permute-start | bytes 1572872 | tf_op jit(solution)/shard_map/ppermute | solution.py:25
  132.1 47.2 %collective-permute-start.6 = (bf16[1,1,512,512]{3,2,0,1:T(8,128)(2,1)S(1)}, bf16[1,1,512,512]{3,2,0,1:T(8,128)(2,1)S(1)}, u32[]{:S(2)}, u32[]{:S(2)}) collective-permute-start(bf16[1,1,512,512]{3,2,0,1:T(8,128)(2,1)S(1)} %bitcast.188), channel_id=1, source_target_pairs={{0,28},{4,0},{8,4},{12,8},{16,12},{20,16},{24,20},{28,24},{1,29},{... | collective-permute-start | bytes 1572872 | tf_op jit(solution)/shard_map/ppermute | solution.py:25
  202.1 8.2 %copy-start.2 = (bf16[96,128,512]{2,1,0:T(8,128)(2,1)S(1)}, bf16[96,128,512]{2,1,0:T(8,128)(2,1)}, u32[]{:S(2)}) copy-start(bf16[96,128,512]{2,1,0:T(8,128)(2,1)} %gather_fusion.7) | copy-start | bytes 37748740
  238.0 5.9 %copy-start.5 = (bf16[1,8,128,512]{3,2,1,0:T(8,128)(2,1)S(1)}, bf16[1,8,128,512]{3,2,1,0:T(8,128)(2,1)}, u32[]{:S(2)}) copy-start(bf16[1,8,128,512]{3,2,1,0:T(8,128)(2,1)} %fusion.5) | copy-start | bytes 3145732
  238.0 5.9 %copy-start.6 = (bf16[1,8,128,512]{3,2,1,0:T(8,128)(2,1)S(1)}, bf16[1,8,128,512]{3,2,1,0:T(8,128)(2,1)}, u32[]{:S(2)}) copy-start(bf16[1,8,128,512]{3,2,1,0:T(8,128)(2,1)} %fusion.6) | copy-start | bytes 3145732
  249.6 103.1 %copy-start.1 = (bf16[16,128,128]{2,1,0:T(8,128)(2,1)S(1)}, bf16[16,128,128]{2,1,0:T(8,128)(2,1)}, u32[]{:S(2)}) copy-start(bf16[16,128,128]{2,1,0:T(8,128)(2,1)} %param.16) | copy-start | bytes 1572868
Sparse Core Ops, SparseCore 0:
  249.8 98.7 reduce-scatter.1
